TPU v7x, 32 devices: a whole 2x2x4 slice. The times are simulated.
32 devices in a mesh: body: 4 (over z), mort: 8 (over y, x, core).
Axes of the slice: x: 2, y: 2, z: 4, core: 2. Of those that a mesh axis runs over, the one named last changes fastest.
Arguments:
- displacement: float32 [3, 64, 256, 128], P(None, 'body', 'mort'), may hold values from -6 to 6
- body_load: float32 [3, 64, 256, 128], P(None, 'body', 'mort'), may hold values from -6 to 6
- stiffness: float32 [64, 256, 128], P('body', 'mort'), may hold values from 0.5 to 4
- initial_gap: float32 [4096, 128], P(('body', 'mort')), may hold values from -6 to 6
- weights: float32 [4096, 128], P(('body', 'mort')), may hold values from 0.05 to 1
- basis_values: float32 [4096, 4, 128], P(('body', 'mort')), may hold values from 0 to 1
- point_cell: int32 [4096, 128], P(('body', 'mort')), may hold values from 0 to 511
- point_segment: int32 [4096, 128], P(('body', 'mort')), may hold values from 0 to 255
- block_owner: int32 [4096, 1], P(('body', 'mort')), may hold values from 0 to 7; in each aligned block of 128 rows (0 to 127, 128 to 255, ...) at most 64 rows name the same one
- multipliers: float32 [4, 8192], P(None, ('body', 'mort')), may hold values from 0 to 2
- block_inverse: float32 [4, 4, 8192], P(None, None, ('body', 'mort')), may hold values from -0.9 to 1
Outputs:
- body_residual: float32 [3, 64, 256, 128], P(None, 'body', 'mort')
- new_multipliers: float32 [4, 8192], P(None, ('body', 'mort'))
Inputs may be any that keep to these rules, and one draw needn't show every extreme that they name: `block_owner`: among the 128 blocks of one device each owner is named at most 64 times.
All inputs are finite; a program needn't handle non-finite values.
Results may differ from a plain program's by a relative error of at most 0.000098.
Values sent between devices are 32-bit elements; how exact they have to be, the bound alone decides.
A program may use at most 128 MiB of HBM per device.

v0:
```python
import math
import jax
import jax.numpy as jnp
from jax import lax
from jax.sharding import PartitionSpec as P

exact = lax.Precision.HIGHEST


def extended(block, sides, width):
    for axis, dim in sides:
        count = lax.axis_size(axis)
        forward = [(i, i + 1) for i in range(count - 1)]
        backward = [(target, source) for source, target in forward]
        low = lax.ppermute(
            lax.slice_in_dim(block, block.shape[dim] - width, None, axis=dim), axis, forward
        )
        high = lax.ppermute(lax.slice_in_dim(block, 0, width, axis=dim), axis, backward)
        block = jnp.concatenate([low, block, high], axis=dim)
    return block


def grouped(fn, arrays, group):
    count = arrays[0].shape[0]
    shaped = tuple((a.reshape((count // group, group) + a.shape[1:]) for a in arrays))
    return lax.map(lambda items: fn(*items), shaped)


def newton_update(integrals, multipliers, block_inverse):
    applied = jnp.sum(block_inverse * integrals[None, :, :], axis=1)
    updated = jnp.maximum(multipliers - applied, 0.0)
    return (updated, updated - multipliers)


def body(
    displacement,
    body_load,
    stiffness,
    initial_gap,
    weights,
    basis_values,
    point_cell,
    point_segment,
    block_owner,
    multipliers,
    block_inverse,
):
    cells_x = displacement.shape[1]
    cells_y = displacement.shape[2]
    blocks = initial_gap.shape[0]
    points = initial_gap.shape[1]
    segments = multipliers.shape[1]
    mort_count = lax.axis_size("mort")
    group = math.gcd(blocks, 16)
    cell_ids = jnp.arange(cells_x * cells_y, dtype=jnp.int32)
    segment_ids_all = jnp.arange(segments, dtype=jnp.int32)
    surface = displacement[2, :, :, 0].reshape(cells_x * cells_y)

    def lookup(cells):
        onehot = (cells[:, :, None] == cell_ids[None, None, :]).astype(jnp.float32)
        return jnp.einsum("gpc,c->gp", onehot, surface, precision=exact)

    point_gap = initial_gap + grouped(lookup, (point_cell,), group).reshape(blocks, points)
    integrand = weights[:, None, :] * basis_values * point_gap[:, None, :]
    owners = block_owner[:, 0]
    owner_onehot = (owners[:, None] == jnp.arange(mort_count, dtype=jnp.int32)[None, :]).astype(
        jnp.float32
    )

    def summed(segs, terms, owner_rows):
        onehot = (segs[:, :, None] == segment_ids_all[None, None, :]).astype(jnp.float32)
        return jnp.einsum("gps,gkp,go->oks", onehot, terms, owner_rows, precision=exact)

    partial_value = jnp.sum(
        grouped(summed, (point_segment, integrand, owner_onehot), group), axis=0
    )
    integrals = lax.psum_scatter(partial_value, "mort", scatter_dimension=0, tiled=True)[0]
    updated, change = newton_update(integrals, multipliers, block_inverse)
    changes = lax.all_gather(change[None], "mort", axis=0, tiled=True)
    block_changes = jnp.einsum("bo,oks->bks", owner_onehot, changes, precision=exact)

    def picked(segs, basis, table):
        onehot = (segs[:, :, None] == segment_ids_all[None, None, :]).astype(jnp.float32)
        return jnp.einsum("gps,gks,gkp->gp", onehot, table, basis, precision=exact)

    pressure = grouped(picked, (point_segment, basis_values, block_changes), group).reshape(
        blocks, points
    )

    def spread(cells, loads):
        onehot = (cells[:, :, None] == cell_ids[None, None, :]).astype(jnp.float32)
        return jnp.einsum("gpc,gp->c", onehot, loads, precision=exact)

    traction = jnp.sum(grouped(spread, (point_cell, weights * pressure), group), axis=0)
    padded = extended(displacement, (("body", 1), ("mort", 2)), 1)
    padded = jnp.pad(padded, ((0, 0), (0, 0), (0, 0), (1, 1)))
    beside = padded[:, 2:, 1:-1, 1:-1] + padded[:, :-2, 1:-1, 1:-1]
    beside = beside + padded[:, 1:-1, 2:, 1:-1] + padded[:, 1:-1, :-2, 1:-1]
    beside = beside + padded[:, 1:-1, 1:-1, 2:] + padded[:, 1:-1, 1:-1, :-2]
    stiff_force = (6.0 + stiffness)[None] * displacement - beside
    residual = body_load - stiff_force
    residual = residual.at[2, :, :, 0].add(traction.reshape(cells_x, cells_y))
    return (residual, updated)


def solution(mesh):
    return jax.shard_map(
        body,
        mesh=mesh,
        in_specs=(
            P(None, "body", "mort", None),
            P(None, "body", "mort", None),
            P("body", "mort", None),
            P(("body", "mort"), None),
            P(("body", "mort"), None),
            P(("body", "mort"), None, None),
            P(("body", "mort"), None),
            P(("body", "mort"), None),
            P(("body", "mort"), None),
            P(None, ("body", "mort")),
            P(None, None, ("body", "mort")),
        ),
        out_specs=(P(None, "body", "mort", None), P(None, ("body", "mort"))),
        check_vma=False,
    )
```

profile of v0, /device:TPU:19, one launch (start us, length us, event | category | flops | bytes accessed | tf_op | source)
XLA Modules:
  0.0 152.1 jit_solution(2052006497745772095)
XLA Ops:
  0.6 0.9 fusion.40
  1.5 3.3 %collective-permute-start.1 = (f32[3,1,32,128]{3,2,1,0:T(8,128)S(1)}, f32[3,1,32,128]{3,2,1,0:T(8,128)S(1)}, u32[]{:S(2)}, u32[]{:S(2)}) collective-permute-start(f32[3,1,32,128]{3,2,1,0:T(8,128)S(1)} %get-tuple-element.245), channel_id=1, source_target_pairs={{0,8},{8,16},{16,24},{1,9},{9,17},{17,25},{2,10},{10,18},{18,26},{... | collective-permute-start | bytes 147464 | tf_op jit(solution)/shard_map/ppermute | solution.py:15
  4.9 2.1 %collective-permute-start = (f32[3,1,32,128]{3,2,1,0:T(8,128)S(1)}, f32[3,1,32,128]{3,2,1,0:T(8,128)S(1)}, u32[]{:S(2)}, u32[]{:S(2)}) collective-permute-start(f32[3,1,32,128]{3,2,1,0:T(8,128)S(1)} %get-tuple-element.244), channel_id=1, source_target_pairs={{8,0},{16,8},{24,16},{9,1},{17,9},{25,17},{10,2},{18,10},{26,18},{... | collective-permute-start | bytes 147464 | tf_op jit(solution)/shard_map/ppermute | solution.py:18
  7.0 1.1 slice_reduce_fusion
  8.2 21.5 %while.45 = (s32[]{:T(128)}, f32[8,16,128]{2,1,0:T(8,128)S(1)}, s32[8,16,128]{2,1,0:T(8,128)}, f32[512]{0:T(512)S(1)}, s32[]{:T(128)}) while((s32[]{:T(128)}, f32[8,16,128]{2,1,0:T(8,128)S(1)}, s32[8,16,128]{2,1,0:T(8,128)}, f32[512]{0:T(512)S(1)}, s32[]{:T(128)}) %tuple.106), condition=%wide.region_1.2_spmd.clone, body=%wide.region_0.1_spmd.clone.sunk | while | flops 13631490 | bytes 51269 | solution.py:26
  8.9 2.0 %fusion.54 = f32[1,16,128]{2,0,1:T(1,128)S(1)} fusion(f32[512,1,1]{0,1,2:T(1,128)S(1)} %bitcast.110, s32[16,128]{1,0:T(8,128)S(1)} %dynamic-slice_bitcast_fusion.9), kind=kOutput, calls=%fused_computation.5.clone.1 | convolution fusion | flops 13631488 | bytes 18432 | tf_op jit(solution)/shard_map/while/body/eval_jaxpr/gpc,c->gp/dot_general | solution.py:61
  10.9 0.7 dynamic-slice_bitcast_fusion.9
  11.6 2.0 %fusion.54 = f32[1,16,128]{2,0,1:T(1,128)S(1)} fusion(f32[512,1,1]{0,1,2:T(1,128)S(1)} %bitcast.110, s32[16,128]{1,0:T(8,128)S(1)} %dynamic-slice_bitcast_fusion.9), kind=kOutput, calls=%fused_computation.5.clone.1 | convolution fusion | flops 13631488 | bytes 18432 | tf_op jit(solution)/shard_map/while/body/eval_jaxpr/gpc,c->gp/dot_general | solution.py:61
  13.6 0.7 dynamic-slice_bitcast_fusion.9
  14.3 2.0 %fusion.54 = f32[1,16,128]{2,0,1:T(1,128)S(1)} fusion(f32[512,1,1]{0,1,2:T(1,128)S(1)} %bitcast.110, s32[16,128]{1,0:T(8,128)S(1)} %dynamic-slice_bitcast_fusion.9), kind=kOutput, calls=%fused_computation.5.clone.1 | convolution fusion | flops 13631488 | bytes 18432 | tf_op jit(solution)/shard_map/while/body/eval_jaxpr/gpc,c->gp/dot_general | solution.py:61
  16.2 0.7 dynamic-slice_bitcast_fusion.9
  17.0 2.0 %fusion.54 = f32[1,16,128]{2,0,1:T(1,128)S(1)} fusion(f32[512,1,1]{0,1,2:T(1,128)S(1)} %bitcast.110, s32[16,128]{1,0:T(8,128)S(1)} %dynamic-slice_bitcast_fusion.9), kind=kOutput, calls=%fused_computation.5.clone.1 | convolution fusion | flops 13631488 | bytes 18432 | tf_op jit(solution)/shard_map/while/body/eval_jaxpr/gpc,c->gp/dot_general | solution.py:61
  18.9 0.7 dynamic-slice_bitcast_fusion.9
  19.6 2.0 %fusion.54 = f32[1,16,128]{2,0,1:T(1,128)S(1)} fusion(f32[512,1,1]{0,1,2:T(1,128)S(1)} %bitcast.110, s32[16,128]{1,0:T(8,128)S(1)} %dynamic-slice_bitcast_fusion.9), kind=kOutput, calls=%fused_computation.5.clone.1 | convolution fusion | flops 13631488 | bytes 18432 | tf_op jit(solution)/shard_map/while/body/eval_jaxpr/gpc,c->gp/dot_general | solution.py:61
  21.6 0.7 dynamic-slice_bitcast_fusion.9
  22.3 2.0 %fusion.54 = f32[1,16,128]{2,0,1:T(1,128)S(1)} fusion(f32[512,1,1]{0,1,2:T(1,128)S(1)} %bitcast.110, s32[16,128]{1,0:T(8,128)S(1)} %dynamic-slice_bitcast_fusion.9), kind=kOutput, calls=%fused_computation.5.clone.1 | convolution fusion | flops 13631488 | bytes 18432 | tf_op jit(solution)/shard_map/while/body/eval_jaxpr/gpc,c->gp/dot_general | solution.py:61
  24.3 0.7 dynamic-slice_bitcast_fusion.9
  25.0 2.0 %fusion.54 = f32[1,16,128]{2,0,1:T(1,128)S(1)} fusion(f32[512,1,1]{0,1,2:T(1,128)S(1)} %bitcast.110, s32[16,128]{1,0:T(8,128)S(1)} %dynamic-slice_bitcast_fusion.9), kind=kOutput, calls=%fused_computation.5.clone.1 | convolution fusion | flops 13631488 | bytes 18432 | tf_op jit(solution)/shard_map/while/body/eval_jaxpr/gpc,c->gp/dot_general | solution.py:61
  27.0 0.7 dynamic-slice_bitcast_fusion.9
  27.7 2.0 %fusion.54 = f32[1,16,128]{2,0,1:T(1,128)S(1)} fusion(f32[512,1,1]{0,1,2:T(1,128)S(1)} %bitcast.110, s32[16,128]{1,0:T(8,128)S(1)} %dynamic-slice_bitcast_fusion.9), kind=kOutput, calls=%fused_computation.5.clone.1 | convolution fusion | flops 13631488 | bytes 18432 | tf_op jit(solution)/shard_map/while/body/eval_jaxpr/gpc,c->gp/dot_general | solution.py:61
  31.1 13.5 %while.46 = (s32[]{:T(128)}, f32[8,8,4,256]{3,1,2,0:T(8,128)S(1)}, f32[8,16,8]{1,2,0:T(8,128)S(1)}, f32[8,16,4,128]{3,2,1,0:T(4,128)S(1)}, s32[8,16,128]{2,1,0:T(8,128)}, /*index=5*/s32[]{:T(128)}) while((s32[]{:T(128)}, f32[8,8,4,256]{3,1,2,0:T(8,128)S(1)}, f32[8,16,8]{1,2,0:T(8,128)S(1)}, f32[8,16,4,128]{3,2,1,0:T(4,128)S(1)}, ...), condition=%wide.region_3.4_spmd.clone, body=%wide.region_2.3_spmd.clone.sunk | while | flops 27262976 | bytes 226381 | solution.py:26
  31.9 0.8 fusion.58
  33.5 0.8 fusion.58
  35.2 0.8 fusion.58
  36.9 0.8 fusion.58
  38.6 0.8 fusion.58
  40.3 0.8 fusion.58
  42.0 0.8 fusion.58
  43.7 0.8 fusion.58
  44.7 21.7 %all-reduce.1 = f32[8,4,256]{2,1,0:T(4,128)S(1)} all-reduce(f32[8,4,256]{2,1,0:T(4,128)S(1)} %copy.33), channel_id=3, replica_groups=mesh['body'=4,'mort'=8] {'mort'}, use_global_device_ids=true, to_apply=%region_5.6.clone | all-reduce | flops 8192 | bytes 65536
  68.2 11.0 %all-gather.1 = f32[8,4,256]{2,1,0:T(4,128)S(1)} all-gather(f32[1,4,256]{2,1,0:T(4,128)S(1)} %get-tuple-element.235), channel_id=2, replica_groups=mesh['body'=4,'mort'=8] {'mort'}, dimensions={0}, use_global_device_ids=true | all-gather | bytes 36864 | tf_op jit(solution)/shard_map/all_gather | solution.py:79
  79.7 14.8 %while.47 = (s32[]{:T(128)}, f32[8,16,128]{2,1,0:T(8,128)S(1)}, f32[8,16,4,128]{3,2,1,0:T(4,128)S(1)}, f32[8,16,4,256]{3,1,0,2:T(8,128)S(1)}, s32[8,16,128]{2,1,0:T(8,128)}, /*index=5*/s32[]{:T(128)}) while((s32[]{:T(128)}, f32[8,16,128]{2,1,0:T(8,128)S(1)}, f32[8,16,4,128]{3,2,1,0:T(4,128)S(1)}, f32[8,16,4,256]{3,1,0,2:T(8,128)S(1)}, ...), condition=%wide.region_8.9_spmd.clone, body=%wide.region_7.8_spmd.clone.sunk | while | flops 25704448 | bytes 278613 | solution.py:26
  80.5 1.1 fusion.60
  81.6 0.7 dynamic-slice_bitcast_fusion.11
  82.3 1.1 fusion.60
  84.2 1.1 fusion.60
  86.0 1.1 fusion.60
  87.9 1.1 fusion.60
  89.7 1.1 fusion.60
  91.6 1.1 fusion.60
  93.4 1.1 fusion.60
  94.6 17.8 %while.48 = (s32[]{:T(128)}, f32[8,512]{1,0:T(8,128)S(1)}, s32[8,16,128]{2,1,0:T(8,128)}, f32[8,16,128]{2,1,0:T(8,128)S(1)}, s32[]{:T(128)}, /*index=5*/s32[]{:T(128)}) while((s32[]{:T(128)}, f32[8,512]{1,0:T(8,128)S(1)}, s32[8,16,128]{2,1,0:T(8,128)}, f32[8,16,128]{2,1,0:T(8,128)S(1)}, s32[]{:T(128)}, ...), condition=%wide.region_10.11_spmd.clone, body=%wide.region_9.10_spmd.clone.sunk | while | flops 13631490 | bytes 55377 | solution.py:26
  94.6 0.8 dynamic-slice_bitcast_fusion.12
  95.4 1.4 fusion.62
  97.6 1.4 fusion.62
  99.8 1.4 fusion.62
  102.0 1.4 fusion.62
  104.3 1.4 fusion.62
  106.5 1.4 fusion.62
  108.7 1.4 fusion.62
  110.9 1.4 fusion.62
  112.5 1.1 pad_maximum_fusion.3
  113.6 2.1 %collective-permute-start.2 = (f32[3,18,1,128]{3,2,1,0:T(1,128)S(1)}, f32[3,18,1,128]{3,2,1,0:T(1,128)S(1)}, u32[]{:S(2)}, u32[]{:S(2)}) collective-permute-start(f32[3,18,1,128]{3,2,1,0:T(1,128)S(1)} %get-tuple-element.240), channel_id=1, source_target_pairs={{1,0},{2,1},{3,2},{4,3},{5,4},{6,5},{7,6},{9,8},{10,9},{11,10},{12... | collective-permute-start | bytes 82952 | tf_op jit(solution)/shard_map/ppermute | solution.py:18
  115.7 4.4 %collective-permute-start.3 = (f32[3,18,1,128]{3,2,1,0:T(1,128)S(1)}, f32[3,18,1,128]{3,2,1,0:T(1,128)S(1)}, u32[]{:S(2)}, u32[]{:S(2)}) collective-permute-start(f32[3,18,1,128]{3,2,1,0:T(1,128)S(1)} %get-tuple-element.239), channel_id=1, source_target_pairs={{0,1},{1,2},{2,3},{3,4},{4,5},{5,6},{6,7},{8,9},{9,10},{10,11},{11... | collective-permute-start | bytes 82952 | tf_op jit(solution)/shard_map/ppermute | solution.py:15
  120.1 2.2 %copy.26 = f32[3,16,32,128]{2,1,3,0:T(8,128)} copy(f32[3,16,32,128]{3,2,1,0:T(8,128)S(1)} %copy-done) | data formatting | bytes 1572864 | tf_op args[0]
  122.4 3.2 %copy.32 = f32[3,16,32,128]{2,1,3,0:T(8,128)} copy(f32[3,16,32,128]{3,2,1,0:T(8,128)} %param.22) | data formatting | bytes 1572864 | tf_op args[1]
  125.6 1.3 copy.25
  127.0 2.2 %copy.46 = f32[3,16,32,128]{2,1,3,0:T(8,128)} copy(f32[3,16,32,128]{3,2,1,0:T(8,128)S(1)} %copy-done.1) | data formatting | bytes 1572864
  129.3 2.2 %copy.47 = f32[3,16,32,128]{2,1,3,0:T(8,128)} copy(f32[3,16,32,128]{3,2,1,0:T(8,128)S(1)} %get-tuple-element.241) | data formatting | bytes 1572864
  131.7 2.3 %copy.48 = f32[3,16,32,128]{2,1,3,0:T(8,128)} copy(f32[3,16,32,128]{3,2,1,0:T(8,128)S(1)} %get-tuple-element.237) | data formatting | bytes 1572864
  134.0 2.3 %copy.49 = f32[3,16,32,128]{2,1,3,0:T(8,128)} copy(f32[3,16,32,128]{3,2,1,0:T(8,128)S(1)} %get-tuple-element.238) | data formatting | bytes 1572864
  136.4 3.4 %copy.31 = f32[3,18,34,128]{2,1,3,0:T(8,128)} copy(f32[3,18,34,128]{3,2,1,0:T(8,128)S(1)} %pad_maximum_fusion) | data formatting | bytes 1880064 | tf_op jit(solution)/shard_map/concatenate | solution.py:19
  139.8 10.4 %fusion.31 = f32[3,16,32,128]{2,1,3,0:T(8,128)S(1)} fusion(f32[3,16,32,128]{2,1,3,0:T(8,128)} %copy.32, f32[3,18,34,128]{2,1,3,0:T(8,128)} %copy.31, f32[3,16,32,128]{2,1,3,0:T(8,128)} %copy.49, f32[3,16,32,128]{2,1,3,0:T(8,128)} %copy.48, f32[3,16,32,128]{2,1,3,0:T(8,128)} %copy.46, f32[3,16,32,128]{2,1,3,0:T(8,128)} %copy.47, f32[3,16,32,128]{2,1,3,0:T(8,128)} %copy.26, ...), kind=kLoop, calls=%fused_computation.43 | loop fusion | flops 1572864 | bytes 6707200 | tf_op jit(solution)/shard_map/sub | solution.py:101
  150.3 1.9 %copy.36 = f32[3,16,32,128]{3,2,1,0:T(8,128)} copy(f32[3,16,32,128]{2,1,3,0:T(8,128)S(1)} %fusion.35) | data formatting | bytes 1572864
  (123 shorter events, 22.5 us)
Async XLA Ops:
  0.6 29.6 %copy-start.8 = (s32[128,1]{0,1:T(1,128)S(1)}, s32[128,1]{0,1:T(1,128)}, u32[]{:S(2)}) copy-start(s32[128,1]{0,1:T(1,128)} %param.29) | copy-start | bytes 1540
  0.6 30.4 %copy-start.5 = (f32[128,128]{1,0:T(8,128)S(1)}, f32[128,128]{1,0:T(8,128)}, u32[]{:S(2)}) copy-start(f32[128,128]{1,0:T(8,128)} %param.24) | copy-start | bytes 196612
  1.5 29.5 %copy-start.2 = (f32[128,128]{1,0:T(8,128)S(1)}, f32[128,128]{1,0:T(8,128)}, u32[]{:S(2)}) copy-start(f32[128,128]{1,0:T(8,128)} %param.25) | copy-start | bytes 196612
  1.5 29.5 %copy-start.3 = (f32[128,4,128]{2,1,0:T(4,128)S(1)}, f32[128,4,128]{2,1,0:T(4,128)}, u32[]{:S(2)}) copy-start(f32[128,4,128]{2,1,0:T(4,128)} %param.26) | copy-start | bytes 786436
  1.5 110.9 %collective-permute-start.1 = (f32[3,1,32,128]{3,2,1,0:T(8,128)S(1)}, f32[3,1,32,128]{3,2,1,0:T(8,128)S(1)}, u32[]{:S(2)}, u32[]{:S(2)}) collective-permute-start(f32[3,1,32,128]{3,2,1,0:T(8,128)S(1)} %get-tuple-element.245), channel_id=1, source_target_pairs={{0,8},{8,16},{16,24},{1,9},{9,17},{17,25},{2,10},{10,18},{18,26},{... | collective-permute-start | bytes 147464 | tf_op jit(solution)/shard_map/ppermute | solution.py:15
  4.9 107.6 %collective-permute-start = (f32[3,1,32,128]{3,2,1,0:T(8,128)S(1)}, f32[3,1,32,128]{3,2,1,0:T(8,128)S(1)}, u32[]{:S(2)}, u32[]{:S(2)}) collective-permute-start(f32[3,1,32,128]{3,2,1,0:T(8,128)S(1)} %get-tuple-element.244), channel_id=1, source_target_pairs={{8,0},{16,8},{24,16},{9,1},{17,9},{25,17},{10,2},{18,10},{26,18},{... | collective-permute-start | bytes 147464 | tf_op jit(solution)/shard_map/ppermute | solution.py:18
  29.7 36.7 %copy-start.9 = (u32[32]{0:T(128)S(1)}, u32[32]{0:T(128)}, u32[]{:S(2)}) copy-start(u32[32]{0:T(128)} %constant.89) | copy-start | bytes 388
  29.7 37.9 %copy-start.6 = (f32[4,4,256]{2,1,0:T(4,128)S(1)}, f32[4,4,256]{2,1,0:T(4,128)}, u32[]{:S(2)}) copy-start(f32[4,4,256]{2,1,0:T(4,128)} %param.31) | copy-start | bytes 49156
  29.7 37.9 %copy-start.7 = (f32[4,256]{1,0:T(4,128)S(1)}, f32[4,256]{1,0:T(4,128)}, u32[]{:S(2)}) copy-start(f32[4,256]{1,0:T(4,128)} %param.30) | copy-start | bytes 12292
  94.6 17.9 %copy-start = (f32[3,16,32,128]{3,2,1,0:T(8,128)S(1)}, f32[3,16,32,128]{3,2,1,0:T(8,128)}, u32[]{:S(2)}) copy-start(f32[3,16,32,128]{3,2,1,0:T(8,128)} %param.21) | copy-start | bytes 2359300
  112.4 7.7 %copy-start.4 = (f32[16,32,128]{2,1,0:T(8,128)S(1)}, f32[16,32,128]{2,1,0:T(8,128)}, u32[]{:S(2)}) copy-start(f32[16,32,128]{2,1,0:T(8,128)} %param.23) | copy-start | bytes 786436
  113.6 17.9 %collective-permute-start.2 = (f32[3,18,1,128]{3,2,1,0:T(1,128)S(1)}, f32[3,18,1,128]{3,2,1,0:T(1,128)S(1)}, u32[]{:S(2)}, u32[]{:S(2)}) collective-permute-start(f32[3,18,1,128]{3,2,1,0:T(1,128)S(1)} %get-tuple-element.240), channel_id=1, source_target_pairs={{1,0},{2,1},{3,2},{4,3},{5,4},{6,5},{7,6},{9,8},{10,9},{11,10},{12... | collective-permute-start | bytes 82952 | tf_op jit(solution)/shard_map/ppermute | solution.py:18
  115.7 15.8 %collective-permute-start.3 = (f32[3,18,1,128]{3,2,1,0:T(1,128)S(1)}, f32[3,18,1,128]{3,2,1,0:T(1,128)S(1)}, u32[]{:S(2)}, u32[]{:S(2)}) collective-permute-start(f32[3,18,1,128]{3,2,1,0:T(1,128)S(1)} %get-tuple-element.239), channel_id=1, source_target_pairs={{0,1},{1,2},{2,3},{3,4},{4,5},{5,6},{6,7},{8,9},{9,10},{10,11},{11... | collective-permute-start | bytes 82952 | tf_op jit(solution)/shard_map/ppermute | solution.py:15
  122.4 4.7 %copy-start.1 = (f32[3,16,32,128]{3,2,1,0:T(8,128)S(1)}, f32[3,16,32,128]{3,2,1,0:T(8,128)}, u32[]{:S(2)}) copy-start(f32[3,16,32,128]{3,2,1,0:T(8,128)} %get-tuple-element.242) | copy-start | bytes 2359300
where the time goes:
time: 154 us; the launch traced here: 152 us
  local copies, waits for them, and re-layouts  48.4 us (31%)
  matrix products  44.1 us (29%)
  blocking collectives  32.7 us (21%)
  other arithmetic  13.4 us (9%)
  starting transfers between devices  11.9 us (8%)
    unnamed x1, blocking collectives  21.7 us
    unnamed x30, local copies, waits for them, and re-layouts  17.5 us
    dot_general x8, matrix products, lookup(): return jnp.einsum('gpc,c->gp', onehot, surface, precision=exact)  15.8 us
    dot_general x8, matrix products, spread(): return jnp.einsum('gpc,gp->c', onehot, loads, precision=exact)  11.5 us
    all_gather x1, blocking collectives, body(): changes = lax.all_gather(change[None], 'mort', axis=0, tiled=True)  11 us
    sub x1, other arithmetic, body(): residual = body_load - stiff_force  10.4 us
    dot_general x8, matrix products, picked(): return jnp.einsum('gps,gks,gkp->gp', onehot, table, basis, precision=exact)  8.74 us
    ppermute x2, starting transfers between devices, extended(): lax.ppermute(lax.slice_in_dim(block, block.shape[dim] - width, None, axis...  7.73 us
  transfers between devices with their start and end apart: 4, of which 0 were waited for; matrix products, arithmetic and copies ran while one was open for 55% of the time, Pallas kernels for 0%

commit v1 on v0

--- a/solution.py
+++ b/solution.py
@@ -76,7 +76,9 @@
     )
     integrals = lax.psum_scatter(partial_value, "mort", scatter_dimension=0, tiled=True)[0]
     updated, change = newton_update(integrals, multipliers, block_inverse)
-    changes = lax.all_gather(change[None], "mort", axis=0, tiled=True)
+    block_2 = change[None]
+    repeated = jnp.stack([block_2] * lax.axis_size("mort"))
+    changes = jnp.concatenate(lax.all_to_all(repeated, "mort", 0, 0), axis=0)
     block_changes = jnp.einsum("bo,oks->bks", owner_onehot, changes, precision=exact)
 
     def picked(segs, basis, table):

time: 154 us -> 150 us (0.974)
  blocking collectives: 32.7 us -> 21.8 us
  starting transfers between devices: 11.9 us -> 18.5 us
    all_gather x1 -> x0, blocking collectives: 11 us -> none  [body(): changes = lax.all_gather(change[None], 'mort', axis=0, tiled=True)]
    all_to_all x0 -> x1, starting transfers between devices: none -> 6.49 us  [body(): changes = jnp.concatenate(lax.all_to_all(repeated, 'mort', 0, 0), axis=0)]
    unnamed x30 -> x32, local copies, waits for them, and re-layouts: 17.5 us -> 16.5 us
  transfers between devices with their start and end apart: 4 -> 5, of which waited for: 0 -> 0; matrix products, arithmetic and copies ran while one was open for 55% -> 56% of each run, Pallas kernels for 0% -> 0%
where the time goes in v1:
time: 150 us; the launch traced here: 147 us
  local copies, waits for them, and re-layouts  48 us (32%)
  matrix products  44.1 us (29%)
  blocking collectives  21.8 us (15%)
  starting transfers between devices  18.5 us (12%)
  other arithmetic  13.4 us (9%)
    unnamed x1, blocking collectives  21.8 us
    unnamed x32, local copies, waits for them, and re-layouts  16.5 us
    dot_general x8, matrix products, lookup(): return jnp.einsum('gpc,c->gp', onehot, surface, precision=exact)  15.8 us
    dot_general x8, matrix products, spread(): return jnp.einsum('gpc,gp->c', onehot, loads, precision=exact)  11.5 us
    sub x1, other arithmetic, body(): residual = body_load - stiff_force  10.4 us
    dot_general x8, matrix products, picked(): return jnp.einsum('gps,gks,gkp->gp', onehot, table, basis, precision=exact)  8.74 us
    dot_general x16, matrix products, summed(): jnp.einsum('gps,gkp,go->oks', onehot, terms, owner_rows, precision=exact)  7.7 us
    ppermute x2, starting transfers between devices, extended(): lax.ppermute(lax.slice_in_dim(block, block.shape[dim] - width, None, axis...  7.5 us
  transfers between devices with their start and end apart: 5, of which 0 were waited for; matrix products, arithmetic and copies ran while one was open for 56% of the time, Pallas kernels for 0%

profile of v1, /device:TPU:19, one launch (start us, length us, event | category | flops | bytes accessed | tf_op | source)
XLA Modules:
  0.0 147.4 jit_solution(814307359335850052)
XLA Ops:
  0.6 0.9 fusion.42
  1.5 3.3 %collective-permute-start.1 = (f32[3,1,32,128]{3,2,1,0:T(8,128)S(1)}, f32[3,1,32,128]{3,2,1,0:T(8,128)S(1)}, u32[]{:S(2)}, u32[]{:S(2)}) collective-permute-start(f32[3,1,32,128]{3,2,1,0:T(8,128)S(1)} %get-tuple-element.245), channel_id=1, source_target_pairs={{0,8},{8,16},{16,24},{1,9},{9,17},{17,25},{2,10},{10,18},{18,26},{... | collective-permute-start | bytes 147464 | tf_op jit(solution)/shard_map/ppermute | solution.py:15
  4.9 2.1 %collective-permute-start = (f32[3,1,32,128]{3,2,1,0:T(8,128)S(1)}, f32[3,1,32,128]{3,2,1,0:T(8,128)S(1)}, u32[]{:S(2)}, u32[]{:S(2)}) collective-permute-start(f32[3,1,32,128]{3,2,1,0:T(8,128)S(1)} %get-tuple-element.244), channel_id=1, source_target_pairs={{8,0},{16,8},{24,16},{9,1},{17,9},{25,17},{10,2},{18,10},{26,18},{... | collective-permute-start | bytes 147464 | tf_op jit(solution)/shard_map/ppermute | solution.py:18
  7.0 1.1 slice_reduce_fusion
  8.2 21.5 %while.45 = (s32[]{:T(128)}, f32[8,16,128]{2,1,0:T(8,128)S(1)}, s32[8,16,128]{2,1,0:T(8,128)}, f32[512]{0:T(512)S(1)}, s32[]{:T(128)}) while((s32[]{:T(128)}, f32[8,16,128]{2,1,0:T(8,128)S(1)}, s32[8,16,128]{2,1,0:T(8,128)}, f32[512]{0:T(512)S(1)}, s32[]{:T(128)}) %tuple.105), condition=%wide.region_1.2_spmd.clone, body=%wide.region_0.1_spmd.clone.sunk | while | flops 13631490 | bytes 51269 | solution.py:26
  8.9 2.0 %fusion.56 = f32[1,16,128]{2,0,1:T(1,128)S(1)} fusion(f32[512,1,1]{0,1,2:T(1,128)S(1)} %bitcast.112, s32[16,128]{1,0:T(8,128)S(1)} %dynamic-slice_bitcast_fusion.9), kind=kOutput, calls=%fused_computation.5.clone.1 | convolution fusion | flops 13631488 | bytes 18432 | tf_op jit(solution)/shard_map/while/body/eval_jaxpr/gpc,c->gp/dot_general | solution.py:61
  10.9 0.7 dynamic-slice_bitcast_fusion.9
  11.6 2.0 %fusion.56 = f32[1,16,128]{2,0,1:T(1,128)S(1)} fusion(f32[512,1,1]{0,1,2:T(1,128)S(1)} %bitcast.112, s32[16,128]{1,0:T(8,128)S(1)} %dynamic-slice_bitcast_fusion.9), kind=kOutput, calls=%fused_computation.5.clone.1 | convolution fusion | flops 13631488 | bytes 18432 | tf_op jit(solution)/shard_map/while/body/eval_jaxpr/gpc,c->gp/dot_general | solution.py:61
  13.5 0.7 dynamic-slice_bitcast_fusion.9
  14.3 2.0 %fusion.56 = f32[1,16,128]{2,0,1:T(1,128)S(1)} fusion(f32[512,1,1]{0,1,2:T(1,128)S(1)} %bitcast.112, s32[16,128]{1,0:T(8,128)S(1)} %dynamic-slice_bitcast_fusion.9), kind=kOutput, calls=%fused_computation.5.clone.1 | convolution fusion | flops 13631488 | bytes 18432 | tf_op jit(solution)/shard_map/while/body/eval_jaxpr/gpc,c->gp/dot_general | solution.py:61
  16.2 0.7 dynamic-slice_bitcast_fusion.9
  16.9 2.0 %fusion.56 = f32[1,16,128]{2,0,1:T(1,128)S(1)} fusion(f32[512,1,1]{0,1,2:T(1,128)S(1)} %bitcast.112, s32[16,128]{1,0:T(8,128)S(1)} %dynamic-slice_bitcast_fusion.9), kind=kOutput, calls=%fused_computation.5.clone.1 | convolution fusion | flops 13631488 | bytes 18432 | tf_op jit(solution)/shard_map/while/body/eval_jaxpr/gpc,c->gp/dot_general | solution.py:61
  18.9 0.7 dynamic-slice_bitcast_fusion.9
  19.6 2.0 %fusion.56 = f32[1,16,128]{2,0,1:T(1,128)S(1)} fusion(f32[512,1,1]{0,1,2:T(1,128)S(1)} %bitcast.112, s32[16,128]{1,0:T(8,128)S(1)} %dynamic-slice_bitcast_fusion.9), kind=kOutput, calls=%fused_computation.5.clone.1 | convolution fusion | flops 13631488 | bytes 18432 | tf_op jit(solution)/shard_map/while/body/eval_jaxpr/gpc,c->gp/dot_general | solution.py:61
  21.6 0.7 dynamic-slice_bitcast_fusion.9
  22.3 2.0 %fusion.56 = f32[1,16,128]{2,0,1:T(1,128)S(1)} fusion(f32[512,1,1]{0,1,2:T(1,128)S(1)} %bitcast.112, s32[16,128]{1,0:T(8,128)S(1)} %dynamic-slice_bitcast_fusion.9), kind=kOutput, calls=%fused_computation.5.clone.1 | convolution fusion | flops 13631488 | bytes 18432 | tf_op jit(solution)/shard_map/while/body/eval_jaxpr/gpc,c->gp/dot_general | solution.py:61
  24.3 0.7 dynamic-slice_bitcast_fusion.9
  25.0 2.0 %fusion.56 = f32[1,16,128]{2,0,1:T(1,128)S(1)} fusion(f32[512,1,1]{0,1,2:T(1,128)S(1)} %bitcast.112, s32[16,128]{1,0:T(8,128)S(1)} %dynamic-slice_bitcast_fusion.9), kind=kOutput, calls=%fused_computation.5.clone.1 | convolution fusion | flops 13631488 | bytes 18432 | tf_op jit(solution)/shard_map/while/body/eval_jaxpr/gpc,c->gp/dot_general | solution.py:61
  27.0 0.7 dynamic-slice_bitcast_fusion.9
  27.7 2.0 %fusion.56 = f32[1,16,128]{2,0,1:T(1,128)S(1)} fusion(f32[512,1,1]{0,1,2:T(1,128)S(1)} %bitcast.112, s32[16,128]{1,0:T(8,128)S(1)} %dynamic-slice_bitcast_fusion.9), kind=kOutput, calls=%fused_computation.5.clone.1 | convolution fusion | flops 13631488 | bytes 18432 | tf_op jit(solution)/shard_map/while/body/eval_jaxpr/gpc,c->gp/dot_general | solution.py:61
  31.2 13.5 %while.46 = (s32[]{:T(128)}, f32[8,8,4,256]{3,1,2,0:T(8,128)S(1)}, f32[8,16,8]{1,2,0:T(8,128)S(1)}, f32[8,16,4,128]{3,2,1,0:T(4,128)S(1)}, s32[8,16,128]{2,1,0:T(8,128)}, /*index=5*/s32[]{:T(128)}) while((s32[]{:T(128)}, f32[8,8,4,256]{3,1,2,0:T(8,128)S(1)}, f32[8,16,8]{1,2,0:T(8,128)S(1)}, f32[8,16,4,128]{3,2,1,0:T(4,128)S(1)}, ...), condition=%wide.region_3.4_spmd.clone, body=%wide.region_2.3_spmd.clone.sunk | while | flops 27262976 | bytes 226381 | solution.py:26
  31.9 0.8 fusion.60
  33.6 0.8 fusion.60
  35.2 0.8 fusion.60
  36.9 0.8 fusion.60
  38.6 0.8 fusion.60
  40.3 0.8 fusion.60
  42.0 0.8 fusion.60
  43.7 0.8 fusion.60
  44.7 21.8 %all-reduce.1 = f32[8,4,256]{2,1,0:T(4,128)S(1)} all-reduce(f32[8,4,256]{2,1,0:T(4,128)S(1)} %copy.33), channel_id=2, replica_groups=mesh['body'=4,'mort'=8] {'mort'}, use_global_device_ids=true, to_apply=%region_5.6.clone | all-reduce | flops 8192 | bytes 65536
  69.0 6.5 %all-to-all-start = ((f32[8,1,4,256]{3,2,1,0:T(4,128)}), f32[8,1,4,256]{3,2,1,0:T(4,128)S(1)}, u32[]{:S(2)}, u32[]{:S(2)}) async-start(f32[8,1,4,256]{3,2,1,0:T(4,128)} %stack.3), calls=%async_computation | async-start | bytes 65536 | tf_op jit(solution)/shard_map/all_to_all | solution.py:81
  75.5 2.2 %copy.26 = f32[3,16,32,128]{2,1,3,0:T(8,128)} copy(f32[3,16,32,128]{3,2,1,0:T(8,128)S(1)} %copy-done) | data formatting | bytes 1572864 | tf_op args[0]
  77.8 2.3 %copy.32 = f32[3,16,32,128]{2,1,3,0:T(8,128)} copy(f32[3,16,32,128]{3,2,1,0:T(8,128)S(1)} %copy-done.2) | data formatting | bytes 1572864 | tf_op args[1]
  80.1 1.4 copy.25
  81.9 14.8 %while.47 = (s32[]{:T(128)}, f32[8,16,128]{2,1,0:T(8,128)S(1)}, f32[8,16,4,128]{3,2,1,0:T(4,128)S(1)}, f32[8,16,4,256]{3,1,2,0:T(8,128)S(1)}, s32[8,16,128]{2,1,0:T(8,128)}, /*index=5*/s32[]{:T(128)}) while((s32[]{:T(128)}, f32[8,16,128]{2,1,0:T(8,128)S(1)}, f32[8,16,4,128]{3,2,1,0:T(4,128)S(1)}, f32[8,16,4,256]{3,1,2,0:T(8,128)S(1)}, ...), condition=%wide.region_8.9_spmd.clone, body=%wide.region_7.8_spmd.clone.sunk | while | flops 25704448 | bytes 278613 | solution.py:26
  81.9 0.7 dynamic-slice_bitcast_fusion.11
  82.6 1.1 fusion.62
  84.4 1.1 fusion.62
  86.3 1.1 fusion.62
  88.2 1.1 fusion.62
  89.3 0.7 dynamic-slice_bitcast_fusion.11
  90.0 1.1 fusion.62
  91.9 1.1 fusion.62
  93.7 1.1 fusion.62
  95.6 1.1 fusion.62
  96.7 1.1 pad_maximum_fusion.3
  97.9 2.4 %collective-permute-start.2 = (f32[3,18,1,128]{3,2,1,0:T(1,128)S(1)}, f32[3,18,1,128]{3,2,1,0:T(1,128)S(1)}, u32[]{:S(2)}, u32[]{:S(2)}) collective-permute-start(f32[3,18,1,128]{3,2,1,0:T(1,128)S(1)} %get-tuple-element.240), channel_id=1, source_target_pairs={{1,0},{2,1},{3,2},{4,3},{5,4},{6,5},{7,6},{9,8},{10,9},{11,10},{12... | collective-permute-start | bytes 82952 | tf_op jit(solution)/shard_map/ppermute | solution.py:18
  100.3 4.2 %collective-permute-start.3 = (f32[3,18,1,128]{3,2,1,0:T(1,128)S(1)}, f32[3,18,1,128]{3,2,1,0:T(1,128)S(1)}, u32[]{:S(2)}, u32[]{:S(2)}) collective-permute-start(f32[3,18,1,128]{3,2,1,0:T(1,128)S(1)} %get-tuple-element.239), channel_id=1, source_target_pairs={{0,1},{1,2},{2,3},{3,4},{4,5},{5,6},{6,7},{8,9},{9,10},{10,11},{11... | collective-permute-start | bytes 82952 | tf_op jit(solution)/shard_map/ppermute | solution.py:15
  104.5 17.7 %while.48 = (s32[]{:T(128)}, f32[8,512]{1,0:T(8,128)S(1)}, s32[8,16,128]{2,1,0:T(8,128)}, f32[8,16,128]{2,1,0:T(8,128)S(1)}, s32[]{:T(128)}, /*index=5*/s32[]{:T(128)}) while((s32[]{:T(128)}, f32[8,512]{1,0:T(8,128)S(1)}, s32[8,16,128]{2,1,0:T(8,128)}, f32[8,16,128]{2,1,0:T(8,128)S(1)}, s32[]{:T(128)}, ...), condition=%wide.region_10.11_spmd.clone, body=%wide.region_9.10_spmd.clone.sunk | while | flops 13631490 | bytes 55377 | solution.py:26
  105.3 1.4 fusion.64
  107.5 1.4 fusion.64
  109.7 1.4 fusion.64
  111.9 1.4 fusion.64
  114.1 1.4 fusion.64
  116.3 1.4 fusion.64
  118.6 1.4 fusion.64
  120.8 1.4 fusion.64
  122.4 2.2 %copy.47 = f32[3,16,32,128]{2,1,3,0:T(8,128)} copy(f32[3,16,32,128]{3,2,1,0:T(8,128)S(1)} %copy-done.1) | data formatting | bytes 1572864
  124.6 2.2 %copy.48 = f32[3,16,32,128]{2,1,3,0:T(8,128)} copy(f32[3,16,32,128]{3,2,1,0:T(8,128)S(1)} %get-tuple-element.241) | data formatting | bytes 1572864
  127.0 2.2 %copy.49 = f32[3,16,32,128]{2,1,3,0:T(8,128)} copy(f32[3,16,32,128]{3,2,1,0:T(8,128)S(1)} %get-tuple-element.237) | data formatting | bytes 1572864
  129.2 2.3 %copy.50 = f32[3,16,32,128]{2,1,3,0:T(8,128)} copy(f32[3,16,32,128]{3,2,1,0:T(8,128)S(1)} %get-tuple-element.238) | data formatting | bytes 1572864
  131.7 3.4 %copy.31 = f32[3,18,34,128]{2,1,3,0:T(8,128)} copy(f32[3,18,34,128]{3,2,1,0:T(8,128)S(1)} %pad_maximum_fusion) | data formatting | bytes 1880064 | tf_op jit(solution)/shard_map/concatenate | solution.py:19
  135.1 10.4 %fusion.31 = f32[3,16,32,128]{2,1,3,0:T(8,128)S(1)} fusion(f32[3,16,32,128]{2,1,3,0:T(8,128)} %copy.32, f32[3,18,34,128]{2,1,3,0:T(8,128)} %copy.31, f32[3,16,32,128]{2,1,3,0:T(8,128)} %copy.50, f32[3,16,32,128]{2,1,3,0:T(8,128)} %copy.49, f32[3,16,32,128]{2,1,3,0:T(8,128)} %copy.47, f32[3,16,32,128]{2,1,3,0:T(8,128)} %copy.48, f32[3,16,32,128]{2,1,3,0:T(8,128)} %copy.26, ...), kind=kLoop, calls=%fused_computation.43 | loop fusion | flops 1572864 | bytes 6707200 | tf_op jit(solution)/shard_map/sub | solution.py:103
  145.5 1.9 %copy.36 = f32[3,16,32,128]{3,2,1,0:T(8,128)} copy(f32[3,16,32,128]{2,1,3,0:T(8,128)S(1)} %fusion.39) | data formatting | bytes 1572864
  (127 shorter events, 23.1 us)
Async XLA Ops:
  0.6 29.6 %copy-start.9 = (s32[128,1]{0,1:T(1,128)S(1)}, s32[128,1]{0,1:T(1,128)}, u32[]{:S(2)}) copy-start(s32[128,1]{0,1:T(1,128)} %param.29) | copy-start | bytes 1540
  0.6 30.4 %copy-start.6 = (f32[128,128]{1,0:T(8,128)S(1)}, f32[128,128]{1,0:T(8,128)}, u32[]{:S(2)}) copy-start(f32[128,128]{1,0:T(8,128)} %param.24) | copy-start | bytes 196612
  1.5 29.5 %copy-start.3 = (f32[128,128]{1,0:T(8,128)S(1)}, f32[128,128]{1,0:T(8,128)}, u32[]{:S(2)}) copy-start(f32[128,128]{1,0:T(8,128)} %param.25) | copy-start | bytes 196612
  1.5 29.5 %copy-start.5 = (f32[128,4,128]{2,1,0:T(4,128)S(1)}, f32[128,4,128]{2,1,0:T(4,128)}, u32[]{:S(2)}) copy-start(f32[128,4,128]{2,1,0:T(4,128)} %param.26) | copy-start | bytes 786436
  1.5 95.2 %collective-permute-start.1 = (f32[3,1,32,128]{3,2,1,0:T(8,128)S(1)}, f32[3,1,32,128]{3,2,1,0:T(8,128)S(1)}, u32[]{:S(2)}, u32[]{:S(2)}) collective-permute-start(f32[3,1,32,128]{3,2,1,0:T(8,128)S(1)} %get-tuple-element.245), channel_id=1, source_target_pairs={{0,8},{8,16},{16,24},{1,9},{9,17},{17,25},{2,10},{10,18},{18,26},{... | collective-permute-start | bytes 147464 | tf_op jit(solution)/shard_map/ppermute | solution.py:15
  4.9 91.9 %collective-permute-start = (f32[3,1,32,128]{3,2,1,0:T(8,128)S(1)}, f32[3,1,32,128]{3,2,1,0:T(8,128)S(1)}, u32[]{:S(2)}, u32[]{:S(2)}) collective-permute-start(f32[3,1,32,128]{3,2,1,0:T(8,128)S(1)} %get-tuple-element.244), channel_id=1, source_target_pairs={{8,0},{16,8},{24,16},{9,1},{17,9},{25,17},{10,2},{18,10},{26,18},{... | collective-permute-start | bytes 147464 | tf_op jit(solution)/shard_map/ppermute | solution.py:18
  29.7 36.8 %copy-start.10 = (u32[32]{0:T(128)S(1)}, u32[32]{0:T(128)}, u32[]{:S(2)}) copy-start(u32[32]{0:T(128)} %constant.89) | copy-start | bytes 388
  29.7 38.1 %copy-start.7 = (f32[4,4,256]{2,1,0:T(4,128)S(1)}, f32[4,4,256]{2,1,0:T(4,128)}, u32[]{:S(2)}) copy-start(f32[4,4,256]{2,1,0:T(4,128)} %param.31) | copy-start | bytes 49156
  29.7 38.1 %copy-start.8 = (f32[4,256]{1,0:T(4,128)S(1)}, f32[4,256]{1,0:T(4,128)}, u32[]{:S(2)}) copy-start(f32[4,256]{1,0:T(4,128)} %param.30) | copy-start | bytes 12292
  29.7 45.8 %copy-start.4 = (f32[16,32,128]{2,1,0:T(8,128)S(1)}, f32[16,32,128]{2,1,0:T(8,128)}, u32[]{:S(2)}) copy-start(f32[16,32,128]{2,1,0:T(8,128)} %param.23) | copy-start | bytes 786436
  29.7 45.8 %copy-start = (f32[3,16,32,128]{3,2,1,0:T(8,128)S(1)}, f32[3,16,32,128]{3,2,1,0:T(8,128)}, u32[]{:S(2)}) copy-start(f32[3,16,32,128]{3,2,1,0:T(8,128)} %param.21) | copy-start | bytes 2359300
  44.7 33.1 %copy-start.2 = (f32[3,16,32,128]{3,2,1,0:T(8,128)S(1)}, f32[3,16,32,128]{3,2,1,0:T(8,128)}, u32[]{:S(2)}) copy-start(f32[3,16,32,128]{3,2,1,0:T(8,128)} %param.22) | copy-start | bytes 2359300
  69.0 12.4 %all-to-all-start = ((f32[8,1,4,256]{3,2,1,0:T(4,128)}), f32[8,1,4,256]{3,2,1,0:T(4,128)S(1)}, u32[]{:S(2)}, u32[]{:S(2)}) async-start(f32[8,1,4,256]{3,2,1,0:T(4,128)} %stack.3), calls=%async_computation | async-start | bytes 65536 | tf_op jit(solution)/shard_map/all_to_all | solution.py:81
  97.9 24.5 %copy-start.1 = (f32[3,16,32,128]{3,2,1,0:T(8,128)S(1)}, f32[3,16,32,128]{3,2,1,0:T(8,128)}, u32[]{:S(2)}) copy-start(f32[3,16,32,128]{3,2,1,0:T(8,128)} %get-tuple-element.242) | copy-start | bytes 2359300
  97.9 28.9 %collective-permute-start.2 = (f32[3,18,1,128]{3,2,1,0:T(1,128)S(1)}, f32[3,18,1,128]{3,2,1,0:T(1,128)S(1)}, u32[]{:S(2)}, u32[]{:S(2)}) collective-permute-start(f32[3,18,1,128]{3,2,1,0:T(1,128)S(1)} %get-tuple-element.240), channel_id=1, source_target_pairs={{1,0},{2,1},{3,2},{4,3},{5,4},{6,5},{7,6},{9,8},{10,9},{11,10},{12... | collective-permute-start | bytes 82952 | tf_op jit(solution)/shard_map/ppermute | solution.py:18
  100.3 26.5 %collective-permute-start.3 = (f32[3,18,1,128]{3,2,1,0:T(1,128)S(1)}, f32[3,18,1,128]{3,2,1,0:T(1,128)S(1)}, u32[]{:S(2)}, u32[]{:S(2)}) collective-permute-start(f32[3,18,1,128]{3,2,1,0:T(1,128)S(1)} %get-tuple-element.239), channel_id=1, source_target_pairs={{0,1},{1,2},{2,3},{3,4},{4,5},{5,6},{6,7},{8,9},{9,10},{10,11},{11... | collective-permute-start | bytes 82952 | tf_op jit(solution)/shard_map/ppermute | solution.py:15
